TPU v7x, 32 devices: a whole 2x2x4 slice. The times are simulated.
32 devices in a mesh: dp: 4 (over z), seq: 8 (over y, x, core).
Axes of the slice: x: 2, y: 2, z: 4, core: 2. Of those that a mesh axis runs over, the one named last changes fastest.
Arguments:
- tiles: bfloat16 [4, 1536, 768], P('dp', 'seq'), may hold values from -40 to 40
- cotangent: bfloat16 [4, 1536, 768], P('dp', 'seq'), may hold values from -0.078125 to 0.078125
- segment_of: int32 [4, 1536, 1], P('dp', 'seq'), may hold values from 0 to 15; in each aligned block of 192 rows (0 to 191, 192 to 383, ..., all dimensions but the last counted through in order) at most 20 rows name the same one
- tissue_count: int32 [4], P('dp'), may hold values from 768 to 1536
- w_query: bfloat16 [768, 768], P('seq'), may hold values from -0.21875 to 0.21875
- w_key: bfloat16 [768, 768], P('seq'), may hold values from -0.21875 to 0.21875
- w_value: bfloat16 [768, 768], P('seq'), may hold values from -0.21875 to 0.21875
- w_out: bfloat16 [768, 768], P('seq'), may hold values from -2.390625 to 2.390625
Outputs:
- layer_out: bfloat16 [4, 1536, 768], P('dp', 'seq')
- grad_value: float32 [768, 768], P('seq')
Inputs may be any that keep to these rules, and one draw needn't show every extreme that they name: `segment_of`: within one slide, the 192 tiles of one block name one group at most 20 times; some group is named exactly 20 times.
All inputs are finite; a program needn't handle non-finite values.
Results may differ from a plain program's by a relative error of at most 0.014.
Values may be sent and summed in bfloat16 or wider, within the bound.
No kernel may reach another device: no remote copies, remote signals or barrier semaphores. Data moves between devices by JAX's collectives and lax.ppermute only.
A program may use at most 64 MiB of HBM per device.

v0:
```python
import jax
import jax.numpy as jnp
from jax import lax
from jax.sharding import PartitionSpec as P

HEADS = 12
SEG_DEV = 2
NEG_BIG = -1e30


def contract_last(left, right):
    return lax.dot_general(
        left, right, (((1,), (1,)), ((), ())), preferred_element_type=jnp.float32
    )


def contract_first(left, right):
    return lax.dot_general(
        left, right, (((0,), (0,)), ((), ())), preferred_element_type=jnp.float32
    )


def local(tiles, cotangent, segment_of, tissue_count, w_query, w_key, w_value, w_out):
    rows = tiles.shape[1]
    width = tiles.shape[2]
    heads = HEADS
    head_dim = width // heads
    scale = head_dim ** (-0.5)
    seq_count = lax.axis_size("seq")
    own_index = lax.axis_index("seq")
    segments = SEG_DEV * seq_count
    capacity = 5 * rows // (3 * segments)
    slots = segments * capacity
    per_segment = seq_count * capacity
    full_query, full_key, full_value, full_out = (
        lax.all_gather(w_query, "seq", axis=0, tiled=True),
        lax.all_gather(w_key, "seq", axis=0, tiled=True),
        lax.all_gather(w_value, "seq", axis=0, tiled=True),
        lax.all_gather(w_out, "seq", axis=0, tiled=True),
    )
    inputs = tiles[0]
    position = own_index * rows + jnp.arange(rows, dtype=jnp.int32)
    inside = position < tissue_count[0]
    masked_cot = cotangent[0] * inside[:, None].astype(jnp.bfloat16)
    query_rows = jnp.dot(inputs, full_query, preferred_element_type=jnp.float32).astype(
        jnp.bfloat16
    )
    key_rows = jnp.dot(inputs, full_key, preferred_element_type=jnp.float32).astype(jnp.bfloat16)
    value_rows = jnp.dot(inputs, full_value, preferred_element_type=jnp.float32).astype(
        jnp.bfloat16
    )
    dout_rows = contract_last(masked_cot, full_out).astype(jnp.bfloat16)

    def by_heads(block):
        return block.reshape(rows, heads, head_dim).transpose(1, 0, 2)

    query_heads = by_heads(query_rows)
    key_heads = by_heads(key_rows)
    visible = inside[None, :] | jnp.eye(rows, dtype=bool)

    def local_scores(query_one, key_one):
        scores = contract_last(query_one, key_one) * scale
        return jnp.where(visible, scores, NEG_BIG)

    def local_stats(pair):
        scores = local_scores(pair[0], pair[1])
        top = jnp.max(scores, axis=1)
        total = jnp.sum(jnp.exp(scores - top[:, None]), axis=1)
        return (top, total)

    local_max, local_sum = lax.map(local_stats, (query_heads, key_heads))
    stats_rows = jnp.stack([local_max.T, local_sum.T], axis=1)
    segment_rows = segment_of[0, :, 0]
    member = (segment_rows[:, None] == jnp.arange(segments, dtype=jnp.int32)[None, :]).astype(
        jnp.int32
    )
    rank = jnp.sum(jnp.cumsum(member, axis=0) * member, axis=1) - 1
    slot_index = segment_rows * capacity + rank
    source_row = (
        jnp.full((slots,), rows, jnp.int32).at[slot_index].set(jnp.arange(rows, dtype=jnp.int32))
    )
    state_rows = jnp.where(inside, 2, 1).astype(jnp.int32)

    def to_slots(block):
        padded = jnp.concatenate([block, jnp.zeros((1,) + block.shape[1:], block.dtype)], axis=0)
        gathered = jnp.take(padded, source_row, axis=0)
        return gathered.reshape((seq_count, SEG_DEV, capacity) + block.shape[1:])

    members = [query_rows, key_rows, value_rows, dout_rows]
    bulk_rows = jnp.stack(members, axis=1)

    def unpack(bulk_one):
        return (bulk_one[:, 0], bulk_one[:, 1], bulk_one[:, 2], bulk_one[:, 3])

    send_bulk = to_slots(bulk_rows)
    send_stats = to_slots(stats_rows)
    send_state = to_slots(state_rows)
    eye_slots = jnp.eye(per_segment, dtype=bool)
    bulk = lax.all_to_all(
        send_bulk.astype(jnp.float32), "seq", split_axis=0, concat_axis=2, tiled=True
    ).astype(send_bulk.dtype)
    stats = lax.all_to_all(send_stats, "seq", split_axis=0, concat_axis=2, tiled=True)
    state = lax.all_to_all(send_state, "seq", split_axis=0, concat_axis=2, tiled=True)

    def one_segment(item):
        bulk_one, stats_one, state_one = item
        query_seg, key_seg, value_seg, dout_seg = unpack(bulk_one)
        slot_count = query_seg.shape[0]
        query_seg = query_seg.reshape(slot_count, heads, head_dim)
        key_seg = key_seg.reshape(slot_count, heads, head_dim)
        value_seg = value_seg.reshape(slot_count, heads, head_dim)
        dout_seg = dout_seg.reshape(slot_count, heads, head_dim)
        seen = (state_one == 2)[None, :] | eye_slots
        scores = (
            jnp.einsum("qhc,khc->hqk", query_seg, key_seg, preferred_element_type=jnp.float32)
            * scale
        )
        scores = jnp.where(seen[None], scores, NEG_BIG)
        far_max = jnp.max(scores, axis=2)
        far_sum = jnp.sum(jnp.exp(scores - far_max[:, :, None]), axis=2)
        seg_near_max = stats_one[:, 0, :].T
        seg_near_sum = stats_one[:, 1, :].T
        top = jnp.maximum(far_max, seg_near_max)
        log_total = top + jnp.log(
            seg_near_sum * jnp.exp(seg_near_max - top) + far_sum * jnp.exp(far_max - top)
        )
        weights = jnp.exp(scores - log_total[:, :, None]).astype(jnp.bfloat16)
        far_out = jnp.einsum("hqk,khc->qhc", weights, value_seg, preferred_element_type=jnp.float32)
        far_grad = jnp.einsum("hqk,qhc->khc", weights, dout_seg, preferred_element_type=jnp.float32)
        far_out = far_out.astype(jnp.bfloat16).reshape(slot_count, width)
        far_grad = far_grad.astype(jnp.bfloat16).reshape(slot_count, width)
        return (far_out, far_grad, log_total.T)

    far_out, far_grad, totals = lax.map(one_segment, (bulk[0], stats[0], state[0]))
    back_bulk = jnp.stack([far_out, far_grad], axis=2)[None]
    back_lse = totals[None]
    home_bulk, home_lse = (
        lax.all_to_all(
            back_bulk.astype(jnp.float32), "seq", split_axis=2, concat_axis=0, tiled=True
        ).astype(back_bulk.dtype),
        lax.all_to_all(back_lse, "seq", split_axis=2, concat_axis=0, tiled=True),
    )
    far_rows = jnp.take(home_bulk.reshape((slots,) + back_bulk.shape[3:]), slot_index, axis=0)
    lse_rows = jnp.take(home_lse.reshape(slots, heads), slot_index, axis=0)

    def local_apply(item):
        query_one, key_one, value_one, dout_one, lse_one = item
        scores = local_scores(query_one, key_one)
        weights = jnp.exp(scores - lse_one[:, None]).astype(jnp.bfloat16)
        near_out = jnp.dot(weights, value_one, preferred_element_type=jnp.float32)
        near_grad = contract_first(weights, dout_one)
        return (near_out, near_grad)

    near_out, near_grad = lax.map(
        local_apply, (query_heads, key_heads, by_heads(value_rows), by_heads(dout_rows), lse_rows.T)
    )
    near_grad = near_grad.transpose(1, 0, 2).reshape(rows, width).astype(jnp.bfloat16)
    far_out_rows = far_rows[:, 0]
    grad_right = far_rows[:, 1]
    attention = (
        near_out.transpose(1, 0, 2).reshape(rows, width) + far_out_rows.astype(jnp.float32)
    ).astype(jnp.bfloat16)
    layer_rows = jnp.dot(attention, full_out, preferred_element_type=jnp.float32).astype(
        jnp.bfloat16
    )
    grad_part = lax.psum_scatter(
        (contract_first(inputs, near_grad) + contract_first(inputs, grad_right)).astype(
            jnp.bfloat16
        ),
        "seq",
        scatter_dimension=0,
        tiled=True,
    ).astype(jnp.float32)
    grad_part = lax.psum(grad_part.astype(jnp.bfloat16), "dp").astype(jnp.float32)
    return (layer_rows[None], grad_part)


def solution(mesh):
    placed = (
        P("dp", "seq", None),
        P("dp", "seq", None),
        P("dp", "seq", None),
        P("dp"),
        P("seq", None),
        P("seq", None),
        P("seq", None),
        P("seq", None),
    )
    return jax.shard_map(
        local,
        mesh=mesh,
        in_specs=placed,
        out_specs=(P("dp", "seq", None), P("seq", None)),
        check_vma=False,
    )
```

profile of v0, /device:TPU:0, one launch (start us, length us, event | category | flops | bytes accessed | tf_op | source)
XLA Modules:
  0.0 328.2 jit_solution(14311517233252371151)
XLA Ops:
  14.5 2.5 gather_fusion.1
  17.6 5.2 %all-to-all-start.1 = ((s32[8,2,20]{2,1,0:T(2,128)}), s32[8,2,20]{2,1,0:T(2,128)S(1)}, u32[]{:S(2)}, u32[]{:S(2)}) async-start(s32[8,2,20]{2,1,0:T(2,128)} %broadcast_select_fusion.2), calls=%async_computation.1 | async-start | bytes 16384 | tf_op jit(solution)/shard_map/all_to_all | solution.py:103
  23.4 13.1 %all-gather.5.cloned.1.call-done = bf16[768,768]{1,0:T(8,128)(2,1)} async-done(((bf16[96,768]{1,0:T(8,128)(2,1)}), bf16[768,768]{1,0:T(8,128)(2,1)}) %all-gather.5.cloned.1.call-update) | async-done | bytes 1179664 | tf_op jit(solution)/shard_map/all_gather | solution.py:36
  36.6 1.7 convolution_convert_fusion.6
  38.7 23.7 %all-gather.7.cloned.1.call-done = bf16[768,768]{1,0:T(8,128)(2,1)} async-done(((bf16[96,768]{1,0:T(8,128)(2,1)}), bf16[768,768]{1,0:T(8,128)(2,1)}) %all-gather.7.cloned.1.call-update) | async-done | bytes 1179664 | tf_op jit(solution)/shard_map/all_gather | solution.py:37
  62.4 1.7 convolution_convert_fusion.5
  64.5 4.9 %while.41 = (s32[]{:T(128)}, f32[12,192]{1,0:T(8,128)S(1)}, f32[12,192]{1,0:T(8,128)S(1)}, bf16[12,192,64]{2,1,0:T(8,128)(2,1)S(1)}, bf16[12,192,64]{2,1,0:T(8,1...) while((s32[]{:T(128)}, f32[12,192]{1,0:T(8,128)S(1)}, ...), condition=%wide.region_7.8_spmd.clone, body=%wide.region_4.7_spmd.clone.sunk | while | flops 4976258 | bytes 400221 | solution.py:71
  70.5 2.0 gather_fusion.2
  73.0 15.2 %all-gather.9.cloned.1.call-done = bf16[768,768]{1,0:T(8,128)(2,1)} async-done(((bf16[96,768]{1,0:T(8,128)(2,1)}), bf16[768,768]{1,0:T(8,128)(2,1)}) %all-gather.9.cloned.1.call-update) | async-done | bytes 1179664 | tf_op jit(solution)/shard_map/all_gather | solution.py:38
  88.2 1.7 convolution_convert_fusion.4
  89.9 24.0 %all-gather.11.cloned.1.call-done = bf16[768,768]{1,0:T(8,128)(2,1)} async-done(((bf16[96,768]{1,0:T(8,128)(2,1)}), bf16[768,768]{1,0:T(8,128)(2,1)}) %all-gather.11.cloned.1.call-update) | async-done | bytes 1179664 | tf_op jit(solution)/shard_map/all_gather | solution.py:39
  113.9 1.8 convolution_convert_fusion.3
  118.9 3.9 %gather_fusion = bf16[320,4,768]{2,1,0:T(4,128)(2,1)S(1)} fusion(bf16[193,4,768]{2,1,0:T(4,128)(2,1)S(1)} %concatenate.16.clone, s32[1024]{0:T(1024)S(1)} %pad_clamp_fusion.1), kind=kCustom, calls=%fused_computation | custom fusion | bytes 3933440 | tf_op jit(solution)/shard_map/jit(_take)/gather | solution.py:86
  122.9 3.3 %all-to-all-start.2 = ((f32[8,1,960]{2,1,0:T(1,128)}), f32[8,1,960]{2,1,0:T(1,128)S(1)}, u32[]{:S(2)}, u32[]{:S(2)}) async-start(f32[8,1,960]{2,1,0:T(1,128)} %reshape.247), calls=%async_computation.2 | async-start | bytes 65536 | tf_op jit(solution)/shard_map/all_to_all | solution.py:102
  126.2 2.1 select_convert_fusion
  128.3 2.6 all-to-all-done.2
  131.0 3.8 %all-to-all-start = ((bf16[8,2,20,4,768]{4,3,2,1,0:T(4,128)(2,1)}), bf16[8,2,20,4,768]{4,3,2,1,0:T(4,128)(2,1)S(1)}, u32[]{:S(2)}, u32[]{:S(2)}) async-start(bf16[8,2,20,4,768]{4,3,2,1,0:T(4,128)(2,1)} %select_convert_fusion), calls=%async_computation | async-start | bytes 3932160 | tf_op jit(solution)/shard_map/all_to_all | solution.py:99
  138.6 21.1 %all-to-all-done = bf16[8,2,20,4,768]{4,3,2,1,0:T(4,128)(2,1)S(1)} async-done(((bf16[8,2,20,4,768]{4,3,2,1,0:T(4,128)(2,1)}), bf16[8,2,20,4,768]{4,3,2,1,0:T(4,128)(2,1)S(1)}, u32[]{:S(2)}, u32[]{:S(2)}) %all-to-all-start) | async-done | bytes 1966112 | tf_op jit(solution)/shard_map/all_to_all | solution.py:99
  159.7 2.0 copy.124
  161.7 11.5 %while.42 = (s32[]{:T(128)}, bf16[2,160,768]{2,1,0:T(8,128)(2,1)}, bf16[2,160,768]{2,1,0:T(8,128)(2,1)}, f32[2,160,12]{1,2,0:T(8,128)S(1)}, bf16[2,160,4,768]{3,...) while((s32[]{:T(128)}, bf16[2,160,768]{2,1,0:T(8,128)(2,1)}, ...), condition=%wide.region_11.12_spmd.clone, body=%wide.region_8.11_spmd.clone.sunk | while | flops 121049760 | bytes 14496293 | solution.py:134
  161.7 1.5 constant_dynamic-slice_fusion.5
  167.4 1.5 constant_dynamic-slice_fusion.5
  174.2 3.3 %all-to-all-start.3 = ((f32[8,1,480]{2,1,0:T(1,128)}), f32[8,1,480]{2,1,0:T(1,128)S(1)}, u32[]{:S(2)}, u32[]{:S(2)}) async-start(f32[8,1,480]{2,1,0:T(1,128)} %reshape.249), calls=%async_computation.3 | async-start | bytes 32768 | tf_op jit(solution)/shard_map/all_to_all | solution.py:141
  178.9 2.0 copy.147
  182.3 4.2 %all-to-all-start.4 = ((bf16[1,2,160,2,768]{4,3,1,0,2:T(2,128)(2,1)}), bf16[1,2,160,2,768]{4,3,1,0,2:T(2,128)(2,1)}, u32[]{:S(2)}, u32[]{:S(2)}) async-start(bf16[1,2,160,2,768]{4,3,1,0,2:T(2,128)(2,1)} %copy.147), calls=%async_computation.4 | async-start | bytes 1966080 | tf_op jit(solution)/shard_map/all_to_all | solution.py:138
  189.1 42.2 %while.43 = (s32[]{:T(128)}, f32[12,192,64]{1,2,0:T(8,128)}, bf16[12,192,64]{1,2,0:T(8,128)(2,1)S(1)}, bf16[12,192,64]{2,1,0:T(8,128)(2,1)}, bf16[12,192,64]{2,1...) while((s32[]{:T(128)}, f32[12,192,64]{1,2,0:T(8,128)}, ...), condition=%wide.region_13.14_spmd.clone, body=%wide.region_12.13_spmd.clone.sunk | while | flops 14376962 | bytes 546345 | solution.py:154
  190.2 1.6 fusion.112
  193.7 1.6 fusion.112
  197.3 1.6 fusion.112
  200.8 1.6 fusion.112
  204.3 1.6 fusion.112
  207.8 1.6 fusion.112
  211.3 1.6 fusion.112
  214.9 1.6 fusion.112
  218.4 1.6 fusion.112
  221.9 1.6 fusion.112
  225.4 1.6 fusion.112
  228.9 1.6 fusion.112
  231.9 1.9 copy.148
  233.8 1.6 copy.149
  235.4 3.1 gather_fusion.4
  239.9 1.6 fusion.46
  241.5 2.4 copy.157
  243.9 1.5 copy.150
  245.4 36.4 %reduce-scatter.4.cloned.1.call-done = bf16[96,768]{1,0:T(8,128)(2,1)} async-done(((bf16[768,768]{1,0:T(8,128)(2,1)}), bf16[96,768]{1,0:T(8,128)(2,1)}) %reduce-scatter.4.cloned.1.call-update) | async-done | bytes 147472
  281.8 1.7 copy.158
  284.7 34.9 %all-reduce.5.cloned.1.call-done = bf16[96,768]{0,1:T(8,128)(2,1)} async-done(((bf16[96,768]{0,1:T(8,128)(2,1)}), bf16[96,768]{0,1:T(8,128)(2,1)}) %all-reduce.5.cloned.1.call-update) | async-done | bytes 147472 | tf_op jit(solution)/shard_map/psum | solution.py:174
  319.6 1.8 copy.151
  (221 shorter events, 62.7 us)
Async XLA Ops:
  7.2 29.4 %copy-start = (bf16[1,192,768]{2,1,0:T(8,128)(2,1)S(1)}, bf16[1,192,768]{2,1,0:T(8,128)(2,1)}, u32[]{:S(2)}) copy-start(bf16[1,192,768]{2,1,0:T(8,128)(2,1)} %param.14) | copy-start | bytes 884740
  7.2 29.4 %all-gather.5.cloned.1.call-start = ((), (), s32[]{:S(2)}) async-start(), calls=%async_computation.6 | async-start | bytes 1327104 | tf_op jit(solution)/shard_map/all_gather | solution.py:36
  7.9 54.5 %all-gather.7.cloned.1.call-start = ((), (), s32[]{:S(2)}) async-start(), calls=%async_computation.7 | async-start | bytes 1327104 | tf_op jit(solution)/shard_map/all_gather | solution.py:37
  8.7 79.6 %all-gather.9.cloned.1.call-start = ((), (), s32[]{:S(2)}) async-start(), calls=%async_computation.8 | async-start | bytes 1327104 | tf_op jit(solution)/shard_map/all_gather | solution.py:38
  17.6 105.2 %all-to-all-start.1 = ((s32[8,2,20]{2,1,0:T(2,128)}), s32[8,2,20]{2,1,0:T(2,128)S(1)}, u32[]{:S(2)}, u32[]{:S(2)}) async-start(s32[8,2,20]{2,1,0:T(2,128)} %broadcast_select_fusion.2), calls=%async_computation.1 | async-start | bytes 16384 | tf_op jit(solution)/shard_map/all_to_all | solution.py:103
  22.8 91.1 %all-gather.11.cloned.1.call-start = ((), (), s32[]{:S(2)}) async-start(), calls=%async_computation.9 | async-start | bytes 1327104 | tf_op jit(solution)/shard_map/all_gather | solution.py:39
  69.4 0.8 copy-start.6
  69.4 3.1 copy-start.7
  70.3 43.6 %copy-start.9 = (bf16[1,192,768]{2,1,0:T(8,128)(2,1)S(1)}, bf16[1,192,768]{2,1,0:T(8,128)(2,1)}, u32[]{:S(2)}) copy-start(bf16[1,192,768]{2,1,0:T(8,128)(2,1)} %param.15) | copy-start | bytes 884740
  89.9 26.7 %copy-start.2 = (bf16[192,768]{1,0:T(8,128)(2,1)}, bf16[192,768]{1,0:T(8,128)(2,1)S(1)}, u32[]{:S(2)}) copy-start(bf16[192,768]{1,0:T(8,128)(2,1)S(1)} %convolution_convert_fusion.4) | copy-start | bytes 884740
  115.7 0.7 copy-start.4
  122.9 8.1 %all-to-all-start.2 = ((f32[8,1,960]{2,1,0:T(1,128)}), f32[8,1,960]{2,1,0:T(1,128)S(1)}, u32[]{:S(2)}, u32[]{:S(2)}) async-start(f32[8,1,960]{2,1,0:T(1,128)} %reshape.247), calls=%async_computation.2 | async-start | bytes 65536 | tf_op jit(solution)/shard_map/all_to_all | solution.py:102
  128.3 6.5 %copy-start.10 = (s32[1,192,1]{1,2,0:T(1,128)S(1)}, s32[1,192,1]{1,2,0:T(1,128)}, u32[]{:S(2)}) copy-start(s32[1,192,1]{1,2,0:T(1,128)} %param.16) | copy-start | bytes 2308
  128.3 6.6 %copy-start.5 = (bf16[192,768]{1,0:T(8,128)(2,1)S(1)}, bf16[192,768]{1,0:T(8,128)(2,1)}, u32[]{:S(2)}) copy-start(bf16[192,768]{1,0:T(8,128)(2,1)} %copy-done.4) | copy-start | bytes 884740
  128.3 7.5 %copy-start.3 = (bf16[192,768]{1,0:T(8,128)(2,1)S(1)}, bf16[192,768]{1,0:T(8,128)(2,1)}, u32[]{:S(2)}) copy-start(bf16[192,768]{1,0:T(8,128)(2,1)} %copy-done.2) | copy-start | bytes 884740
  131.0 28.7 %all-to-all-start = ((bf16[8,2,20,4,768]{4,3,2,1,0:T(4,128)(2,1)}), bf16[8,2,20,4,768]{4,3,2,1,0:T(4,128)(2,1)S(1)}, u32[]{:S(2)}, u32[]{:S(2)}) async-start(bf16[8,2,20,4,768]{4,3,2,1,0:T(4,128)(2,1)} %select_convert_fusion), calls=%async_computation | async-start | bytes 3932160 | tf_op jit(solution)/shard_map/all_to_all | solution.py:99
  174.2 8.0 %all-to-all-start.3 = ((f32[8,1,480]{2,1,0:T(1,128)}), f32[8,1,480]{2,1,0:T(1,128)S(1)}, u32[]{:S(2)}, u32[]{:S(2)}) async-start(f32[8,1,480]{2,1,0:T(1,128)} %reshape.249), calls=%async_computation.3 | async-start | bytes 32768 | tf_op jit(solution)/shard_map/all_to_all | solution.py:141
  180.9 8.3 %copy-start.8 = (bf16[12,192,64]{1,2,0:T(8,128)(2,1)S(1)}, bf16[12,192,64]{1,2,0:T(8,128)(2,1)}, u32[]{:S(2)}) copy-start(bf16[12,192,64]{1,2,0:T(8,128)(2,1)} %custom-call.16) | copy-start | bytes 884740
  182.3 49.6 %all-to-all-start.4 = ((bf16[1,2,160,2,768]{4,3,1,0,2:T(2,128)(2,1)}), bf16[1,2,160,2,768]{4,3,1,0,2:T(2,128)(2,1)}, u32[]{:S(2)}, u32[]{:S(2)}) async-start(bf16[1,2,160,2,768]{4,3,1,0,2:T(2,128)(2,1)} %copy.147), calls=%async_computation.4 | async-start | bytes 1966080 | tf_op jit(solution)/shard_map/all_to_all | solution.py:138
  186.5 95.3 %reduce-scatter.4.cloned.1.call-start = ((), (), s32[]{:S(2)}) async-start(), calls=%async_computation.11 | async-start | bytes 1327104
  243.8 39.7 %copy-start.1 = (bf16[768,768]{1,0:T(8,128)(2,1)S(1)}, bf16[768,768]{1,0:T(8,128)(2,1)}, u32[]{:S(2)}) copy-start(bf16[768,768]{1,0:T(8,128)(2,1)} %all-gather.11.cloned.1.call-done) | copy-start | bytes 3538948
  243.9 75.7 %all-reduce.5.cloned.1.call-start = ((), (), s32[]{:S(2)}) async-start(), calls=%async_computation.10 | async-start | bytes 393216 | tf_op jit(solution)/shard_map/psum | solution.py:174
Sparse Core Ops, SparseCore 0:
  9.9 26.6 all-gather.4
  38.4 23.9 all-gather.6
  64.3 23.9 all-gather.8
  90.0 23.9 all-gather.10
  244.0 37.7 reduce-scatter.3
  284.5 34.9 all-reduce.4
where the time goes:
time: 331 us; the launch traced here: 328 us
  waiting for transfers between devices  175 us (53%)
  matrix products  57.6 us (17%)
  local copies, waits for them, and re-layouts  47.3 us (14%)
  starting transfers between devices  20.3 us (6%)
  between operations  15.3 us (5%)
  other arithmetic  11.8 us (4%)
    unnamed x7, waiting for transfers between devices  39 us
    psum x1, waiting for transfers between devices, local(): lax.psum(grad_part.astype(jnp.bfloat16), 'dp').astype(jnp.float32)  34.9 us
    all_gather x1, waiting for transfers between devices, local(): lax.all_gather(w_out, 'seq', axis=0, tiled=True)  24 us
    all_gather x1, waiting for transfers between devices, local(): lax.all_gather(w_key, 'seq', axis=0, tiled=True)  23.7 us
    all_to_all x1, waiting for transfers between devices, local(): lax.all_to_all(send_bulk.astype(jnp.float32), 'seq', split_axis=0, concat...  21.1 us
    dot_general x12, matrix products, local_apply(): near_out = jnp.dot(weights, value_one, preferred_element_type=jnp.float32)  18.6 us
    dot_general x25, matrix products, contract_last(): lax.dot_general(left, right, (((1,), (1,)), ((), ())), preferred_element_...  17.2 us
    all_gather x1, waiting for transfers between devices, local(): lax.all_gather(w_value, 'seq', axis=0, tiled=True)  15.2 us
  transfers between devices with their start and end apart: 11, of which 9 were waited for; matrix products, arithmetic and copies ran while one was open for 26% of the time, Pallas kernels for 0%

commit v1 on v0

--- a/solution.py
+++ b/solution.py
@@ -96,8 +96,14 @@
     send_stats = to_slots(stats_rows)
     send_state = to_slots(state_rows)
     eye_slots = jnp.eye(per_segment, dtype=bool)
-    bulk = lax.all_to_all(
-        send_bulk.astype(jnp.float32), "seq", split_axis=0, concat_axis=2, tiled=True
+    bulk = jnp.concatenate(
+        lax.all_to_all(
+            jnp.stack(jnp.split(send_bulk.astype(jnp.float32), lax.axis_size("seq"), axis=0)),
+            "seq",
+            0,
+            0,
+        ),
+        axis=2,
     ).astype(send_bulk.dtype)
     stats = lax.all_to_all(send_stats, "seq", split_axis=0, concat_axis=2, tiled=True)
     state = lax.all_to_all(send_state, "seq", split_axis=0, concat_axis=2, tiled=True)

time: 331 us -> 362 us (1.094)
  waiting for transfers between devices: 175 us -> 185 us
  matrix products: 57.6 us -> 67.1 us
  local copies, waits for them, and re-layouts: 47.3 us -> 56.5 us
    dot_general x25, matrix products: 17.2 us -> 26.8 us  [contract_last(): lax.dot_general(left, right, (((1,), (1,)), ((), ())), preferred_element_...]
    all_gather x1, waiting for transfers between devices: 15.2 us -> 23.2 us  [local(): lax.all_gather(w_value, 'seq', axis=0, tiled=True)]
    unnamed x36 -> x33, local copies, waits for them, and re-layouts: 11.5 us -> 18 us
  transfers between devices with their start and end apart: 11 -> 11, of which waited for: 9 -> 9; matrix products, arithmetic and copies ran while one was open for 26% -> 30% of each run, Pallas kernels for 0% -> 0%
where the time goes in v1:
time: 362 us; the launch traced here: 358 us
  waiting for transfers between devices  185 us (51%)
  matrix products  67.1 us (19%)
  local copies, waits for them, and re-layouts  56.5 us (16%)
  starting transfers between devices  20.3 us (6%)
  between operations  15.2 us (4%)
  other arithmetic  13 us (4%)
    unnamed x7, waiting for transfers between devices  39 us
    psum x1, waiting for transfers between devices, local(): lax.psum(grad_part.astype(jnp.bfloat16), 'dp').astype(jnp.float32)  34.9 us
    dot_general x25, matrix products, contract_last(): lax.dot_general(left, right, (((1,), (1,)), ((), ())), preferred_element_...  26.8 us
    all_gather x1, waiting for transfers between devices, local(): lax.all_gather(w_out, 'seq', axis=0, tiled=True)  24 us
    all_gather x1, waiting for transfers between devices, local(): lax.all_gather(w_key, 'seq', axis=0, tiled=True)  24 us
    all_gather x1, waiting for transfers between devices, local(): lax.all_gather(w_value, 'seq', axis=0, tiled=True)  23.2 us
    all_to_all x1, waiting for transfers between devices, local(): lax.all_to_all(jnp.stack(jnp.split(send_bulk.astype(jnp.float32), lax.axi...  21.2 us
    dot_general x12, matrix products, local_apply(): near_out = jnp.dot(weights, value_one, preferred_element_type=jnp.float32)  18.7 us
  transfers between devices with their start and end apart: 11, of which 9 were waited for; matrix products, arithmetic and copies ran while one was open for 30% of the time, Pallas kernels for 0%

profile of v1, /device:TPU:0, one launch (start us, length us, event | category | flops | bytes accessed | tf_op | source)
XLA Modules:
  0.0 357.6 jit_solution(16604011389781454952)
XLA Ops:
  15.0 2.5 gather_fusion.1
  18.2 5.2 %all-to-all-start.1 = ((s32[8,2,20]{2,1,0:T(2,128)}), s32[8,2,20]{2,1,0:T(2,128)S(1)}, u32[]{:S(2)}, u32[]{:S(2)}) async-start(s32[8,2,20]{2,1,0:T(2,128)} %broadcast_select_fusion.2), calls=%async_computation.1 | async-start | bytes 16384 | tf_op jit(solution)/shard_map/all_to_all | solution.py:109
  23.4 13.1 %all-gather.5.cloned.1.call-done = bf16[768,768]{1,0:T(8,128)(2,1)} async-done(((bf16[96,768]{1,0:T(8,128)(2,1)}), bf16[768,768]{1,0:T(8,128)(2,1)}) %all-gather.5.cloned.1.call-update) | async-done | bytes 1179664 | tf_op jit(solution)/shard_map/all_gather | solution.py:36
  36.6 1.7 convolution_convert_fusion.6
  38.4 24.0 %all-gather.7.cloned.1.call-done = bf16[768,768]{1,0:T(8,128)(2,1)} async-done(((bf16[96,768]{1,0:T(8,128)(2,1)}), bf16[768,768]{1,0:T(8,128)(2,1)}) %all-gather.7.cloned.1.call-update) | async-done | bytes 1179664 | tf_op jit(solution)/shard_map/all_gather | solution.py:37
  62.4 1.7 convolution_convert_fusion.5
  65.0 23.2 %all-gather.9.cloned.1.call-done = bf16[768,768]{1,0:T(8,128)(2,1)} async-done(((bf16[96,768]{1,0:T(8,128)(2,1)}), bf16[768,768]{1,0:T(8,128)(2,1)}) %all-gather.9.cloned.1.call-update) | async-done | bytes 1179664 | tf_op jit(solution)/shard_map/all_gather | solution.py:38
  88.2 1.7 convolution_convert_fusion.4
  89.9 24.0 %all-gather.11.cloned.1.call-done = bf16[768,768]{1,0:T(8,128)(2,1)} async-done(((bf16[96,768]{1,0:T(8,128)(2,1)}), bf16[768,768]{1,0:T(8,128)(2,1)}) %all-gather.11.cloned.1.call-update) | async-done | bytes 1179664 | tf_op jit(solution)/shard_map/all_gather | solution.py:39
  113.9 1.8 convolution_convert_fusion.3
  117.3 4.4 %gather_fusion = bf16[320,4,768]{2,1,0:T(4,128)(2,1)} fusion(bf16[193,4,768]{2,1,0:T(4,128)(2,1)S(1)} %concatenate.16.clone, s32[1024]{0:T(1024)S(1)} %get-tuple-element.352), kind=kCustom, calls=%fused_computation | custom fusion | bytes 3933440 | tf_op jit(solution)/shard_map/jit(_take)/gather | solution.py:86
  121.7 2.4 select_convert_fusion
  131.9 14.4 %while.41 = (s32[]{:T(128)}, f32[12,192]{1,0:T(8,128)S(1)}, f32[12,192]{1,0:T(8,128)S(1)}, bf16[12,192,64]{2,1,0:T(8,128)(2,1)}, bf16[12,192,64]{2,1,0:T(8,128)(...) while((s32[]{:T(128)}, f32[12,192]{1,0:T(8,128)S(1)}, f32[12,192]{1,0:T(8,128)S(1)}, ...), condition=%wide.region_7.8_spmd.clone, body=%wide.region_4.7_spmd.clone.sunk | while | flops 4976258 | bytes 400221 | solution.py:71
  147.4 2.0 gather_fusion.2
  152.3 3.3 all-to-all-start.2
  156.5 4.0 %all-to-all-done.2 = f32[8,1,960]{2,1,0:T(1,128)S(1)} async-done(((f32[8,1,960]{2,1,0:T(1,128)}), f32[8,1,960]{2,1,0:T(1,128)S(1)}, u32[]{:S(2)}, u32[]{:S(2)}) %all-to-all-start.2) | async-done | bytes 30752 | tf_op jit(solution)/shard_map/all_to_all | solution.py:108
  160.5 3.8 %all-to-all-start = ((bf16[8,1,2,20,4,768]{5,4,3,2,1,0:T(4,128)(2,1)}), bf16[8,1,2,20,4,768]{5,4,3,2,1,0:T(4,128)(2,1)S(1)}, u32[]{:S(2)}, u32[]{:S(2)}) async-start(bf16[8,1,2,20,4,768]{5,4,3,2,1,0:T(4,128)(2,1)} %fusion.49), calls=%async_computation | async-start | bytes 3932160 | tf_op jit(solution)/shard_map/all_to_all | solution.py:100
  168.0 21.2 %all-to-all-done = bf16[8,1,2,20,4,768]{5,4,3,2,1,0:T(4,128)(2,1)S(1)} async-done(((bf16[8,1,2,20,4,768]{5,4,3,2,1,0:T(4,128)(2,1)}), bf16[8,1,2,20,4,768]{5,4,3,2,1,0:T(4,128)(2,1)S(1)}, u32[]{:S(2)}, u32[]{:S(2)}) %all-to-all-start) | async-done | bytes 1966112 | tf_op jit(solution)/shard_map/all_to_all | solution.py:100
  189.2 2.0 copy.131
  191.2 11.5 %while.42 = (s32[]{:T(128)}, bf16[2,160,768]{2,1,0:T(8,128)(2,1)}, bf16[2,160,768]{2,1,0:T(8,128)(2,1)}, f32[2,160,12]{1,2,0:T(8,128)S(1)}, bf16[2,160,4,768]{3,...) while((s32[]{:T(128)}, bf16[2,160,768]{2,1,0:T(8,128)(2,1)}, ...), condition=%wide.region_11.12_spmd.clone, body=%wide.region_8.11_spmd.clone.sunk | while | flops 121049760 | bytes 14496293 | solution.py:140
  191.2 1.5 constant_dynamic-slice_fusion.5
  196.9 1.5 constant_dynamic-slice_fusion.5
  203.7 3.3 all-to-all-start.3
  208.3 2.0 copy.154
  211.7 4.2 %all-to-all-start.4 = ((bf16[1,2,160,2,768]{4,3,1,0,2:T(2,128)(2,1)}), bf16[1,2,160,2,768]{4,3,1,0,2:T(2,128)(2,1)}, u32[]{:S(2)}, u32[]{:S(2)}) async-start(bf16[1,2,160,2,768]{4,3,1,0,2:T(2,128)(2,1)} %copy.154), calls=%async_computation.4 | async-start | bytes 1966080 | tf_op jit(solution)/shard_map/all_to_all | solution.py:144
  218.6 42.2 %while.43 = (s32[]{:T(128)}, f32[12,192,64]{1,2,0:T(8,128)}, bf16[12,192,64]{1,2,0:T(8,128)(2,1)S(1)}, bf16[12,192,64]{2,1,0:T(8,128)(2,1)}, bf16[12,192,64]{2,1...) while((s32[]{:T(128)}, f32[12,192,64]{1,2,0:T(8,128)}, ...), condition=%wide.region_13.14_spmd.clone, body=%wide.region_12.13_spmd.clone.sunk | while | flops 14376962 | bytes 546345 | solution.py:160
  219.6 1.6 fusion.120
  223.2 1.6 fusion.120
  226.7 1.6 fusion.120
  230.2 1.6 fusion.120
  233.7 1.6 fusion.120
  237.3 1.6 fusion.120
  240.8 1.6 fusion.120
  244.3 1.6 fusion.120
  247.8 1.6 fusion.120
  251.3 1.6 fusion.120
  254.9 1.6 fusion.120
  258.4 1.6 fusion.120
  261.3 1.9 copy.155
  263.2 1.6 copy.156
  264.8 3.1 gather_fusion.4
  269.4 1.6 fusion.46
  270.9 2.4 copy.164
  273.4 1.5 copy.157
  274.8 36.4 %reduce-scatter.4.cloned.1.call-done = bf16[96,768]{1,0:T(8,128)(2,1)} async-done(((bf16[768,768]{1,0:T(8,128)(2,1)}), bf16[96,768]{1,0:T(8,128)(2,1)}) %reduce-scatter.4.cloned.1.call-update) | async-done | bytes 147472
  311.3 1.7 copy.165
  314.1 34.9 %all-reduce.5.cloned.1.call-done = bf16[96,768]{0,1:T(8,128)(2,1)} async-done(((bf16[96,768]{0,1:T(8,128)(2,1)}), bf16[96,768]{0,1:T(8,128)(2,1)}) %all-reduce.5.cloned.1.call-update) | async-done | bytes 147472 | tf_op jit(solution)/shard_map/psum | solution.py:180
  349.0 1.8 copy.158
  (218 shorter events, 81.8 us)
Async XLA Ops:
  7.2 29.4 %copy-start = (bf16[1,192,768]{2,1,0:T(8,128)(2,1)S(1)}, bf16[1,192,768]{2,1,0:T(8,128)(2,1)}, u32[]{:S(2)}) copy-start(bf16[1,192,768]{2,1,0:T(8,128)(2,1)} %param.14) | copy-start | bytes 884740
  7.2 29.4 %all-gather.5.cloned.1.call-start = ((), (), s32[]{:S(2)}) async-start(), calls=%async_computation.6 | async-start | bytes 1327104 | tf_op jit(solution)/shard_map/all_gather | solution.py:36
  7.9 54.5 %all-gather.7.cloned.1.call-start = ((), (), s32[]{:S(2)}) async-start(), calls=%async_computation.7 | async-start | bytes 1327104 | tf_op jit(solution)/shard_map/all_gather | solution.py:37
  8.7 79.6 %all-gather.9.cloned.1.call-start = ((), (), s32[]{:S(2)}) async-start(), calls=%async_computation.8 | async-start | bytes 1327104 | tf_op jit(solution)/shard_map/all_gather | solution.py:38
  9.4 104.5 %all-gather.11.cloned.1.call-start = ((), (), s32[]{:S(2)}) async-start(), calls=%async_computation.9 | async-start | bytes 1327104 | tf_op jit(solution)/shard_map/all_gather | solution.py:39
  18.2 134.1 %all-to-all-start.1 = ((s32[8,2,20]{2,1,0:T(2,128)}), s32[8,2,20]{2,1,0:T(2,128)S(1)}, u32[]{:S(2)}, u32[]{:S(2)}) async-start(s32[8,2,20]{2,1,0:T(2,128)} %broadcast_select_fusion.2), calls=%async_computation.1 | async-start | bytes 16384 | tf_op jit(solution)/shard_map/all_to_all | solution.py:109
  38.4 75.5 %copy-start.4 = (bf16[1,192,768]{2,1,0:T(8,128)(2,1)S(1)}, bf16[1,192,768]{2,1,0:T(8,128)(2,1)}, u32[]{:S(2)}) copy-start(bf16[1,192,768]{2,1,0:T(8,128)(2,1)} %param.15) | copy-start | bytes 884740
  146.3 0.8 copy-start.2
  152.3 8.1 %all-to-all-start.2 = ((f32[8,1,960]{2,1,0:T(1,128)}), f32[8,1,960]{2,1,0:T(1,128)S(1)}, u32[]{:S(2)}, u32[]{:S(2)}) async-start(f32[8,1,960]{2,1,0:T(1,128)} %reshape.248), calls=%async_computation.2 | async-start | bytes 65536 | tf_op jit(solution)/shard_map/all_to_all | solution.py:108
  156.5 7.8 %copy-start.5 = (s32[1,192,1]{1,2,0:T(1,128)S(1)}, s32[1,192,1]{1,2,0:T(1,128)}, u32[]{:S(2)}) copy-start(s32[1,192,1]{1,2,0:T(1,128)} %param.16) | copy-start | bytes 2308
  160.5 28.7 %all-to-all-start = ((bf16[8,1,2,20,4,768]{5,4,3,2,1,0:T(4,128)(2,1)}), bf16[8,1,2,20,4,768]{5,4,3,2,1,0:T(4,128)(2,1)S(1)}, u32[]{:S(2)}, u32[]{:S(2)}) async-start(bf16[8,1,2,20,4,768]{5,4,3,2,1,0:T(4,128)(2,1)} %fusion.49), calls=%async_computation | async-start | bytes 3932160 | tf_op jit(solution)/shard_map/all_to_all | solution.py:100
  203.7 8.0 %all-to-all-start.3 = ((f32[8,1,480]{2,1,0:T(1,128)}), f32[8,1,480]{2,1,0:T(1,128)S(1)}, u32[]{:S(2)}, u32[]{:S(2)}) async-start(f32[8,1,480]{2,1,0:T(1,128)} %reshape.250), calls=%async_computation.3 | async-start | bytes 32768 | tf_op jit(solution)/shard_map/all_to_all | solution.py:147
  210.3 8.3 %copy-start.3 = (bf16[12,192,64]{1,2,0:T(8,128)(2,1)S(1)}, bf16[12,192,64]{1,2,0:T(8,128)(2,1)}, u32[]{:S(2)}) copy-start(bf16[12,192,64]{1,2,0:T(8,128)(2,1)} %custom-call.17) | copy-start | bytes 884740
  211.7 49.6 %all-to-all-start.4 = ((bf16[1,2,160,2,768]{4,3,1,0,2:T(2,128)(2,1)}), bf16[1,2,160,2,768]{4,3,1,0,2:T(2,128)(2,1)}, u32[]{:S(2)}, u32[]{:S(2)}) async-start(bf16[1,2,160,2,768]{4,3,1,0,2:T(2,128)(2,1)} %copy.154), calls=%async_computation.4 | async-start | bytes 1966080 | tf_op jit(solution)/shard_map/all_to_all | solution.py:144
  215.9 95.3 %reduce-scatter.4.cloned.1.call-start = ((), (), s32[]{:S(2)}) async-start(), calls=%async_computation.11 | async-start | bytes 1327104
  273.3 39.7 %copy-start.1 = (bf16[768,768]{1,0:T(8,128)(2,1)S(1)}, bf16[768,768]{1,0:T(8,128)(2,1)}, u32[]{:S(2)}) copy-start(bf16[768,768]{1,0:T(8,128)(2,1)} %all-gather.11.cloned.1.call-done) | copy-start | bytes 3538948
  273.3 75.7 %all-reduce.5.cloned.1.call-start = ((), (), s32[]{:S(2)}) async-start(), calls=%async_computation.10 | async-start | bytes 393216 | tf_op jit(solution)/shard_map/psum | solution.py:180
Sparse Core Ops, SparseCore 0:
  9.9 26.6 all-gather.4
  38.4 23.9 all-gather.6
  64.3 23.9 all-gather.8
  90.0 23.9 all-gather.10
  273.4 37.7 reduce-scatter.3
  314.0 34.9 all-reduce.4
